TPU v7x, 512 devices: a whole 4x4x16 slice. The times are simulated.
512 devices in a mesh: blk: 16 (over z), pen: 32 (over x, y, core).
Axes of the slice: x: 4, y: 4, z: 16, core: 2. Of those that a mesh axis runs over, the one named last changes fastest.
Arguments:
- state: bfloat16 [16, 2, 32, 512, 512], P('blk', None, None, 'pen'), may hold values from -6 to 6
- inverse_x: bfloat16 [16, 2, 512, 512], P('blk')
- inverse_y: bfloat16 [16, 2, 512, 512], P('blk')
- rates: float32 [16, 3], P('blk'), may hold values from 0.05 to 0.4
- partner: int32 [16, 2], P('blk'), may hold values from 0 to 15
- face_side: int32 [16, 2], P('blk'), may hold values from 0 to 1
- orient: int32 [16, 2], P('blk'), may hold values from 0 to 1
- offset: int32 [16, 2], P('blk'), may hold values from 0 to 31
Outputs:
- relaxed: bfloat16 [16, 2, 32, 512, 512], P('blk', None, None, 'pen')
All inputs are finite; a program needn't handle non-finite values.
Results may differ from a plain program's by a relative error of at most 0.0058.
Values may be sent and summed in bfloat16 or wider, within the bound.
No kernel may reach another device: no remote copies, remote signals or barrier semaphores. Data moves between devices by JAX's collectives and lax.ppermute only.
A program may use at most 64 MiB of HBM per device.

v0:
```python
import jax
import jax.numpy as jnp
from jax import lax
from jax.sharding import PartitionSpec as P

STEPS = 2


def plane_ghosts(layers, partner_row, side_row, orient_row, offset_row, tile_rows):
    blocks = lax.all_gather(layers[None], "blk", axis=0, tiled=True)
    lines = layers.shape[-1]
    rows_y = jnp.arange(lines, dtype=jnp.int32)
    result = []
    for which in range(2):
        piece = lax.dynamic_index_in_dim(blocks, partner_row[which], 0, keepdims=False)
        segment = lax.dynamic_index_in_dim(piece, side_row[which], 0, keepdims=False)
        mirrored = jnp.where(orient_row[which] == 1, lines - 1 - rows_y, rows_y)
        take_at = (mirrored + offset_row[which] * tile_rows) % lines
        result.append(jnp.take(segment, take_at, axis=-1))
    return result


def local(state, inverse_x, inverse_y, rates, partner, face_side, orient, offset):
    magnet = state[0]
    inv_x = inverse_x[0]
    inv_y = inverse_y[0]
    rate_row = rates[0]
    first_col = inv_x[:, :, 0].astype(jnp.float32)
    last_col = inv_x[:, :, -1].astype(jnp.float32)
    tile_rows = magnet.shape[2]
    planes = lax.all_to_all(magnet, "pen", split_axis=1, concat_axis=2, tiled=True)
    for repeat in range(STEPS):
        layers = jnp.stack([planes[..., 0], planes[..., -1]], axis=0)
        ghosts = plane_ghosts(layers, partner[0], face_side[0], orient[0], offset[0], tile_rows)
        interior = jnp.einsum("fax,fzyx->fzya", inv_x, planes, preferred_element_type=jnp.float32)
        edges = first_col[:, None, None, :] * ghosts[0].astype(jnp.float32)[..., None]
        edges = edges + last_col[:, None, None, :] * ghosts[1].astype(jnp.float32)[..., None]
        swept_x = (interior + edges).astype(jnp.bfloat16)
        swept_y = jnp.einsum("fcy,fzyx->fzcx", inv_y, swept_x, preferred_element_type=jnp.float32)
        proton = swept_y[0]
        carbon = swept_y[1]
        new_proton = proton - (rate_row[0] * proton + rate_row[2] * carbon)
        new_carbon = carbon - (rate_row[1] * carbon + rate_row[2] * proton)
        planes = jnp.stack([new_proton, new_carbon]).astype(jnp.bfloat16)
    magnet = lax.all_to_all(planes, "pen", split_axis=2, concat_axis=1, tiled=True)
    return magnet[None]


def solution(mesh):
    return jax.shard_map(
        local,
        mesh=mesh,
        in_specs=(
            P("blk", None, None, "pen", None),
            P("blk", None, None, None),
            P("blk", None, None, None),
            P("blk", None),
            P("blk", None),
            P("blk", None),
            P("blk", None),
            P("blk", None),
        ),
        out_specs=P("blk", None, None, "pen", None),
        check_vma=False,
    )
```

profile of v0, /device:TPU:1, one launch (start us, length us, event | category | flops | bytes accessed | tf_op | source)
XLA Modules:
  0.0 137.5 jit_solution(13616519110712983959)
XLA Ops:
  0.1 2.4 %copy.81 = bf16[1,2,32,16,512]{4,3,1,2,0:T(8,128)(2,1)} copy(bf16[1,2,32,16,512]{4,3,2,1,0:T(8,128)(2,1)} %param.10) | data formatting | bytes 2097152 | tf_op args[0]
  2.5 10.5 %all-to-all-start = ((bf16[2,32,16,512]{3,2,0,1:T(8,128)(2,1)}), bf16[2,32,16,512]{3,2,0,1:T(8,128)(2,1)S(1)}, u32[]{:S(2)}, u32[]{:S(2)}) async-start(bf16[2,32,16,512]{3,2,0,1:T(8,128)(2,1)} %bitcast.95), calls=%async_computation | async-start | bytes 2097152 | tf_op jit(solution)/shard_map/all_to_all | solution.py:31
  13.0 0.6 fusion.19
  16.1 0.6 fusion.18
  21.5 0.6 fusion.16
  23.4 0.7 fusion.17
  25.5 0.7 fusion.15
  26.2 0.3 convert_reduce_fusion.1
  26.5 3.5 %all-to-all-done = bf16[2,32,16,512]{3,2,0,1:T(8,128)(2,1)S(1)} async-done(((bf16[2,32,16,512]{3,2,0,1:T(8,128)(2,1)}), bf16[2,32,16,512]{3,2,0,1:T(8,128)(2,1)S(1)}, u32[]{:S(2)}, u32[]{:S(2)}) %all-to-all-start) | async-done | bytes 1048608 | tf_op jit(solution)/shard_map/all_to_all | solution.py:31
  30.0 0.3 slice_reduce_fusion.1
  30.4 26.5 %all-gather = bf16[32,2,1,512]{3,1,2,0:T(2,128)(2,1)S(1)} all-gather(bf16[2,2,1,512]{3,1,2,0:T(2,128)(2,1)S(1)} %pad_maximum_fusion.3), channel_id=2, replica_groups=mesh['blk'=16,'pen'=32] {'blk'}, dimensions={0}, use_global_device_ids=true | all-gather | bytes 69632 | tf_op jit(solution)/shard_map/all_gather | solution.py:10
  56.9 0.2 copy.74
  57.1 1.3 gather_fusion
  58.5 0.1 bitcast_convert_fusion.3
  58.6 0.1 copy.57
  58.7 0.2 copy.75
  58.9 1.3 gather_fusion.1
  60.3 0.1 bitcast_convert_fusion.2
  60.5 4.0 %convolution_bitcast_fusion.1 = f32[2,1,512,512]{2,3,0,1:T(8,128)} fusion(bf16[1,2,512,512]{3,2,1,0:T(8,128)(2,1)S(1)} %copy-done, bf16[2,512,512]{2,1,0:T(8,128)(2,1)S(1)} %bitcast.97, f32[2,512]{1,0:T(2,128)S(1)} %copy.59, f32[2,512]{1,0:T(2,128)S(1)} %get-tuple-element.7, f32[2,512]{1,0:T(2,128)S(1)} %copy.57, f32[2,512]{1,0:T(2,128)S(1)} %get-tuple-element.6, ...), kind=kOutput, calls=%fused_computation.7 | convolution fusion | flops 1076363264 | bytes 5259264 | tf_op jit(solution)/shard_map/fcy,fzyx->fzcx/dot_general | solution.py:39
  64.5 3.8 %subtract_convert_fusion.3 = (bf16[1,1,512,512]{2,3,0,1:T(8,128)(2,1)S(1)}, bf16[1,1,512,512]{2,3,0,1:T(8,128)(2,1)S(1)}) fusion(f32[2,1,512,512]{2,3,0,1:T(8,128)} %convolution_bitcast_fusion.1, f32[]{:T(128)} %bitcast.27, f32[]{:T(128)} %bitcast.26, f32[]{:T(128)} %bitcast.30), kind=kLoop, calls=%fused_computation.18 | loop fusion | flops 2621440 | bytes 3145740 | tf_op jit(solution)/shard_map/convert.13
  68.3 19.7 %all-gather.1 = bf16[32,2,1,512]{3,1,2,0:T(2,128)(2,1)S(1)} all-gather(bf16[2,2,1,512]{3,1,2,0:T(2,128)(2,1)S(1)} %pad_maximum_fusion.4), channel_id=3, replica_groups=mesh['blk'=16,'pen'=32] {'blk'}, dimensions={0}, use_global_device_ids=true | all-gather | bytes 69632 | tf_op jit(solution)/shard_map/all_gather | solution.py:10
  88.1 0.2 copy.76
  88.3 1.3 gather_fusion.2
  89.6 0.7 bitcast_convert_fusion.1
  90.5 0.2 copy.77
  90.7 1.3 gather_fusion.3
  92.0 0.7 bitcast_convert_fusion
  92.9 3.9 %convolution_bitcast_fusion = f32[2,1,512,512]{2,3,0,1:T(8,128)} fusion(bf16[1,2,512,512]{3,2,1,0:T(8,128)(2,1)S(1)} %copy-done, bf16[1,512,512]{1,2,0:T(8,128)(2,1)S(1)} %bitcast.99, bf16[1,512,512]{1,2,0:T(8,128)(2,1)S(1)} %bitcast.98, f32[2,512]{1,0:T(2,128)S(1)} %copy.65, f32[2,512]{1,0:T(2,128)S(1)} %copy.63, f32[2,512]{1,0:T(2,128)} %copy-done.4, ...), kind=kOutput, calls=%fused_computation.6 | convolution fusion | flops 1076887552 | bytes 5259264 | tf_op jit(solution)/shard_map/fcy,fzyx->fzcx/dot_general | solution.py:39
  96.8 3.8 %subtract_convert_fusion.1 = (bf16[1,1,512,512]{2,3,0,1:T(8,128)(2,1)S(1)}, bf16[1,1,512,512]{2,3,0,1:T(8,128)(2,1)S(1)}) fusion(f32[2,1,512,512]{2,3,0,1:T(8,128)} %convolution_bitcast_fusion, f32[]{:T(128)} %bitcast.27, f32[]{:T(128)} %bitcast.26, f32[]{:T(128)} %bitcast.30), kind=kLoop, calls=%fused_computation.16 | loop fusion | flops 2621440 | bytes 3145740 | tf_op jit(solution)/shard_map/convert.6
  100.7 1.0 copy.67
  101.7 34.6 %all_to_all.21 = bf16[2,1,512,512]{3,0,1,2:T(2,128)(2,1)S(1)} all-to-all(bf16[2,1,512,512]{3,0,1,2:T(2,128)(2,1)S(1)} %copy.67), channel_id=1, replica_groups=mesh['blk'=16,'pen'=32] {'pen'}, dimensions={2} | all-to-all | bytes 2097152 | tf_op jit(solution)/shard_map/all_to_all | solution.py:45
  136.3 1.1 copy.68
  (39 shorter events, 0.7 us)
Async XLA Ops:
  0.0 60.5 %copy-start = (bf16[1,2,512,512]{3,2,1,0:T(8,128)(2,1)S(1)}, bf16[1,2,512,512]{3,2,1,0:T(8,128)(2,1)}, u32[]{:S(2)}) copy-start(bf16[1,2,512,512]{3,2,1,0:T(8,128)(2,1)} %param.12) | copy-start | bytes 3145732
  0.0 12.9 %copy-start.7 = (s32[1,2]{1,0:T(1,128)S(1)}, s32[1,2]{1,0:T(1,128)}, u32[]{:S(2)}) copy-start(s32[1,2]{1,0:T(1,128)} %param.14) | copy-start | bytes 28
  0.0 16.1 %copy-start.8 = (s32[1,2]{1,0:T(1,128)S(1)}, s32[1,2]{1,0:T(1,128)}, u32[]{:S(2)}) copy-start(s32[1,2]{1,0:T(1,128)} %param.15) | copy-start | bytes 28
  0.0 21.5 %copy-start.9 = (s32[1,2]{1,0:T(1,128)S(1)}, s32[1,2]{1,0:T(1,128)}, u32[]{:S(2)}) copy-start(s32[1,2]{1,0:T(1,128)} %param.16) | copy-start | bytes 28
  0.0 23.3 %copy-start.10 = (s32[1,2]{1,0:T(1,128)S(1)}, s32[1,2]{1,0:T(1,128)}, u32[]{:S(2)}) copy-start(s32[1,2]{1,0:T(1,128)} %param.17) | copy-start | bytes 28
  0.0 25.5 %copy-start.3 = (f32[1,3]{1,0:T(1,128)S(1)}, f32[1,3]{1,0:T(1,128)}, u32[]{:S(2)}) copy-start(f32[1,3]{1,0:T(1,128)} %param.13) | copy-start | bytes 40
  0.0 26.1 %copy-start.1 = (bf16[1,2,512,512]{3,2,1,0:T(8,128)(2,1)S(1)}, bf16[1,2,512,512]{3,2,1,0:T(8,128)(2,1)}, u32[]{:S(2)}) copy-start(bf16[1,2,512,512]{3,2,1,0:T(8,128)(2,1)} %param.11) | copy-start | bytes 3145732
  2.5 27.5 %all-to-all-start = ((bf16[2,32,16,512]{3,2,0,1:T(8,128)(2,1)}), bf16[2,32,16,512]{3,2,0,1:T(8,128)(2,1)S(1)}, u32[]{:S(2)}, u32[]{:S(2)}) async-start(bf16[2,32,16,512]{3,2,0,1:T(8,128)(2,1)} %bitcast.95), calls=%async_computation | async-start | bytes 2097152 | tf_op jit(solution)/shard_map/all_to_all | solution.py:31
  25.4 33.5 %copy-start.6 = (pred[512]{0:T(512)(128)(4,1)}, pred[512]{0:T(512)(128)(4,1)S(1)}, u32[]{:S(2)}) copy-start(pred[512]{0:T(512)(128)(4,1)S(1)} %compare_and_fusion.1) | copy-start | bytes 1540
  25.4 34.8 %copy-start.5 = (pred[512]{0:T(512)(128)(4,1)}, pred[512]{0:T(512)(128)(4,1)S(1)}, u32[]{:S(2)}) copy-start(pred[512]{0:T(512)(128)(4,1)S(1)} %compare_and_fusion) | copy-start | bytes 1540
  26.5 34.0 %copy-start.4 = (f32[2,512]{1,0:T(2,128)}, f32[2,512]{1,0:T(2,128)S(1)}, u32[]{:S(2)}) copy-start(f32[2,512]{1,0:T(2,128)S(1)} %get-tuple-element.7) | copy-start | bytes 12292
  68.3 24.6 %copy-start.2 = (bf16[1,2,512,512]{3,2,1,0:T(8,128)(2,1)S(1)}, bf16[1,2,512,512]{3,2,1,0:T(8,128)(2,1)}, u32[]{:S(2)}) copy-start(bf16[1,2,512,512]{3,2,1,0:T(8,128)(2,1)} %param.11) | copy-start | bytes 3145732
where the time goes:
time: 138 us; the launch traced here: 137 us
  blocking collectives  80.9 us (59%)
  local copies, waits for them, and re-layouts  14.7 us (11%)
  starting transfers between devices  10.5 us (8%)
  between operations  10.2 us (7%)
  other arithmetic  9.87 us (7%)
  matrix products  7.85 us (6%)
  waiting for transfers between devices  3.45 us (2%)
    all_gather x2, blocking collectives, plane_ghosts(): blocks = lax.all_gather(layers[None], 'blk', axis=0, tiled=True)  46.3 us
    all_to_all x1, blocking collectives, local(): lax.all_to_all(planes, 'pen', split_axis=2, concat_axis=1, tiled=True)  34.6 us
    all_to_all x1, starting transfers between devices, local(): lax.all_to_all(magnet, 'pen', split_axis=1, concat_axis=2, tiled=True)  10.5 us
    dot_general x2, matrix products, local(): jnp.einsum('fcy,fzyx->fzcx', inv_y, swept_x, preferred_element_type=jnp.f...  7.85 us
    another operation x2, other arithmetic  7.59 us
    gather x4, local copies, waits for them, and re-layouts, plane_ghosts(): result.append(jnp.take(segment, take_at, axis=-1))  5.36 us
    all_to_all x1, waiting for transfers between devices, local(): lax.all_to_all(magnet, 'pen', split_axis=1, concat_axis=2, tiled=True)  3.45 us
    unnamed x28, local copies, waits for them, and re-layouts  3.23 us
  transfers between devices with their start and end apart: 1, of which 1 were waited for; matrix products, arithmetic and copies ran while one was open for 3% of the time, Pallas kernels for 0%

commit v1 on v0

--- a/solution.py
+++ b/solution.py
@@ -7,7 +7,9 @@
 
 
 def plane_ghosts(layers, partner_row, side_row, orient_row, offset_row, tile_rows):
-    blocks = lax.all_gather(layers[None], "blk", axis=0, tiled=True)
+    blocks = jnp.concatenate(
+        lax.all_to_all(jnp.stack([layers[None]] * lax.axis_size("blk")), "blk", 0, 0), axis=0
+    )
     lines = layers.shape[-1]
     rows_y = jnp.arange(lines, dtype=jnp.int32)
     result = []

time: 138 us -> 120 us (0.87)
  blocking collectives: 80.9 us -> 37.9 us
  starting transfers between devices: 10.5 us -> 23.4 us
  waiting for transfers between devices: 3.45 us -> 14 us
    all_gather x2 -> x0, blocking collectives: 46.3 us -> none  [plane_ghosts(): blocks = lax.all_gather(layers[None], 'blk', axis=0, tiled=True)]
    all_to_all x0 -> x1, blocking collectives: none -> 15.5 us  [plane_ghosts(): lax.all_to_all(jnp.stack([layers[None]] * lax.axis_size('blk')), 'blk', 0...]
    all_to_all x0 -> x1, starting transfers between devices: none -> 13 us  [plane_ghosts(): lax.all_to_all(jnp.stack([layers[None]] * lax.axis_size('blk')), 'blk', 0...]
    all_to_all x1, blocking collectives: 34.6 us -> 22.5 us  [local(): lax.all_to_all(planes, 'pen', split_axis=2, concat_axis=1, tiled=True)]
    all_to_all x0 -> x1, waiting for transfers between devices: none -> 10.2 us  [plane_ghosts(): lax.all_to_all(jnp.stack([layers[None]] * lax.axis_size('blk')), 'blk', 0...]
    unnamed x28 -> x22, local copies, waits for them, and re-layouts: 3.23 us -> 2.42 us
  transfers between devices with their start and end apart: 1 -> 2, of which waited for: 1 -> 2; matrix products, arithmetic and copies ran while one was open for 3% -> 4% of each run, Pallas kernels for 0% -> 0%
where the time goes in v1:
time: 120 us
  blocking collectives  37.9 us (32%)
  starting transfers between devices  23.4 us (20%)
  local copies, waits for them, and re-layouts  15.3 us (13%)
  waiting for transfers between devices  14 us (12%)
  other arithmetic  10.9 us (9%)
  between operations  10.2 us (8%)
  matrix products  7.86 us (7%)
    all_to_all x1, blocking collectives, local(): lax.all_to_all(planes, 'pen', split_axis=2, concat_axis=1, tiled=True)  22.5 us
    all_to_all x1, blocking collectives, plane_ghosts(): lax.all_to_all(jnp.stack([layers[None]] * lax.axis_size('blk')), 'blk', 0...  15.5 us
    all_to_all x1, starting transfers between devices, plane_ghosts(): lax.all_to_all(jnp.stack([layers[None]] * lax.axis_size('blk')), 'blk', 0...  13 us
    all_to_all x1, starting transfers between devices, local(): lax.all_to_all(magnet, 'pen', split_axis=1, concat_axis=2, tiled=True)  10.5 us
    all_to_all x1, waiting for transfers between devices, plane_ghosts(): lax.all_to_all(jnp.stack([layers[None]] * lax.axis_size('blk')), 'blk', 0...  10.2 us
    dot_general x2, matrix products, local(): jnp.einsum('fcy,fzyx->fzcx', inv_y, swept_x, preferred_element_type=jnp.f...  7.86 us
    another operation x2, other arithmetic  7.49 us
    gather x4, local copies, waits for them, and re-layouts, plane_ghosts(): result.append(jnp.take(segment, take_at, axis=-1))  5.36 us
  transfers between devices with their start and end apart: 2, of which 2 were waited for; matrix products, arithmetic and copies ran while one was open for 4% of the time, Pallas kernels for 0%

profile of v1, /device:TPU:1, one launch (start us, length us, event | category | flops | bytes accessed | tf_op | source)
XLA Modules:
  0.0 119.7 jit_solution(8040975433714026391)
XLA Ops:
  0.0 2.4 %copy.70 = bf16[1,2,32,16,512]{4,3,1,2,0:T(8,128)(2,1)} copy(bf16[1,2,32,16,512]{4,3,2,1,0:T(8,128)(2,1)} %param.10) | data formatting | bytes 2097152 | tf_op args[0]
  2.4 10.5 %all-to-all-start = ((bf16[2,32,16,512]{3,2,0,1:T(8,128)(2,1)}), bf16[2,32,16,512]{3,2,0,1:T(8,128)(2,1)S(1)}, u32[]{:S(2)}, u32[]{:S(2)}) async-start(bf16[2,32,16,512]{3,2,0,1:T(8,128)(2,1)} %bitcast.97), calls=%async_computation | async-start | bytes 2097152 | tf_op jit(solution)/shard_map/all_to_all | solution.py:33
  12.9 0.6 fusion.19
  16.0 0.7 fusion.18
  21.7 0.6 fusion.16
  23.4 0.7 fusion.17
  25.4 0.7 fusion.15
  26.1 3.8 %all-to-all-done = bf16[2,32,16,512]{3,2,0,1:T(8,128)(2,1)S(1)} async-done(((bf16[2,32,16,512]{3,2,0,1:T(8,128)(2,1)}), bf16[2,32,16,512]{3,2,0,1:T(8,128)(2,1)S(1)}, u32[]{:S(2)}, u32[]{:S(2)}) %all-to-all-start) | async-done | bytes 1048608 | tf_op jit(solution)/shard_map/all_to_all | solution.py:33
  30.0 0.3 slice_reduce_fusion.1
  30.3 0.7 stack.34
  31.0 13.0 %all-to-all-start.1 = ((bf16[16,1,2,2,1,512]{5,3,4,2,1,0:T(2,128)(2,1)}), bf16[16,1,2,2,1,512]{5,3,4,2,1,0:T(2,128)(2,1)S(1)}, u32[]{:S(2)}, u32[]{:S(2)}) async-start(bf16[16,1,2,2,1,512]{5,3,4,2,1,0:T(2,128)(2,1)} %stack.34), calls=%async_computation.1 | async-start | bytes 131072 | tf_op jit(solution)/shard_map/all_to_all | solution.py:11
  44.0 1.3 %convert_reduce_fusion.1 = (f32[2,512]{1,0:T(2,128)S(1)}, f32[2,512]{1,0:T(2,128)S(1)}) fusion(bf16[2,512,512]{2,1,0:T(8,128)(2,1)} %bitcast.102), kind=kLoop, calls=%fused_computation.20 | loop fusion | flops 2048 | bytes 12288 | tf_op jit(solution)/shard_map/convert_element_type | solution.py:30
  45.3 10.2 %all-to-all-done.1 = bf16[16,1,2,2,1,512]{5,3,4,2,1,0:T(2,128)(2,1)S(1)} async-done(((bf16[16,1,2,2,1,512]{5,3,4,2,1,0:T(2,128)(2,1)}), bf16[16,1,2,2,1,512]{5,3,4,2,1,0:T(2,128)(2,1)S(1)}, u32[]{:S(2)}, u32[]{:S(2)}) %all-to-all-start.1) | async-done | bytes 65568 | tf_op jit(solution)/shard_map/all_to_all | solution.py:11
  55.6 0.2 copy.49
  55.8 1.3 %gather_fusion = bf16[512,2]{1,0:T(8,128)(2,1)S(1)} fusion(bf16[2,512]{0,1:T(8,128)(2,1)S(1)} %bitcast.105, s32[1024]{0:T(1024)S(1)} %pad_clamp_fusion.1), kind=kCustom, calls=%fused_computation.clone | custom fusion | bytes 6144 | tf_op jit(solution)/shard_map/jit(_take)/gather | solution.py:21
  57.4 0.2 copy.51
  57.6 1.3 %gather_fusion.1 = bf16[512,2]{1,0:T(8,128)(2,1)S(1)} fusion(bf16[2,512]{0,1:T(8,128)(2,1)S(1)} %bitcast.106, s32[1024]{0:T(1024)S(1)} %pad_clamp_fusion), kind=kCustom, calls=%fused_computation.1.clone | custom fusion | bytes 6144 | tf_op jit(solution)/shard_map/jit(_take)/gather | solution.py:21
  58.9 0.1 bitcast_convert_fusion.2
  59.2 4.0 %convolution_bitcast_fusion.1 = f32[2,1,512,512]{2,3,0,1:T(8,128)} fusion(bf16[1,2,512,512]{3,2,1,0:T(8,128)(2,1)S(1)} %copy-done, bf16[2,512,512]{2,1,0:T(8,128)(2,1)S(1)} %bitcast.99, f32[2,512]{1,0:T(2,128)S(1)} %copy.52, f32[2,512]{1,0:T(2,128)S(1)} %get-tuple-element.7, f32[2,512]{1,0:T(2,128)S(1)} %copy.50, f32[2,512]{1,0:T(2,128)S(1)} %get-tuple-element.6, ...), kind=kOutput, calls=%fused_computation.7 | convolution fusion | flops 1076363264 | bytes 5259264 | tf_op jit(solution)/shard_map/fcy,fzyx->fzcx/dot_general | solution.py:41
  63.1 3.7 %subtract_convert_fusion.3 = (bf16[1,1,512,512]{2,3,0,1:T(8,128)(2,1)S(1)}, bf16[1,1,512,512]{2,3,0,1:T(8,128)(2,1)S(1)}) fusion(f32[2,1,512,512]{2,3,0,1:T(8,128)} %convolution_bitcast_fusion.1, f32[]{:T(128)} %bitcast.27, f32[]{:T(128)} %bitcast.26, f32[]{:T(128)} %bitcast.30), kind=kLoop, calls=%fused_computation.18 | loop fusion | flops 2621440 | bytes 3145740 | tf_op jit(solution)/shard_map/convert.13
  67.0 15.5 %all_to_all.31 = bf16[16,1,2,2,1,512]{5,3,4,2,1,0:T(2,128)(2,1)S(1)} all-to-all(bf16[16,1,2,2,1,512]{5,3,4,2,1,0:T(2,128)(2,1)S(1)} %stack.41), channel_id=1, replica_groups=mesh['blk'=16,'pen'=32] {'blk'}, dimensions={0} | all-to-all | bytes 131072 | tf_op jit(solution)/shard_map/all_to_all | solution.py:11
  82.5 0.2 copy.55
  82.7 1.3 %gather_fusion.2 = bf16[512,2]{1,0:T(8,128)(2,1)S(1)} fusion(bf16[2,512]{0,1:T(8,128)(2,1)S(1)} %bitcast.103, s32[1024]{0:T(1024)S(1)} %pad_clamp_fusion.1), kind=kCustom, calls=%fused_computation.2.clone | custom fusion | bytes 6144 | tf_op jit(solution)/shard_map/jit(_take)/gather | solution.py:21
  84.0 0.8 bitcast_convert_fusion.1
  84.9 0.2 copy.57
  85.1 1.3 %gather_fusion.3 = bf16[512,2]{1,0:T(8,128)(2,1)S(1)} fusion(bf16[2,512]{0,1:T(8,128)(2,1)S(1)} %bitcast.104, s32[1024]{0:T(1024)S(1)} %pad_clamp_fusion), kind=kCustom, calls=%fused_computation.3.clone | custom fusion | bytes 6144 | tf_op jit(solution)/shard_map/jit(_take)/gather | solution.py:21
  86.5 0.7 bitcast_convert_fusion
  87.3 3.9 %convolution_bitcast_fusion = f32[2,1,512,512]{2,3,0,1:T(8,128)} fusion(bf16[1,2,512,512]{3,2,1,0:T(8,128)(2,1)S(1)} %copy-done, bf16[1,512,512]{1,2,0:T(8,128)(2,1)S(1)} %bitcast.101, bf16[1,512,512]{1,2,0:T(8,128)(2,1)S(1)} %bitcast.100, f32[2,512]{1,0:T(2,128)S(1)} %copy.58, f32[2,512]{1,0:T(2,128)S(1)} %copy.56, f32[2,512]{1,0:T(2,128)} %copy-done.3, ...), kind=kOutput, calls=%fused_computation.6 | convolution fusion | flops 1076887552 | bytes 5259264 | tf_op jit(solution)/shard_map/fcy,fzyx->fzcx/dot_general | solution.py:41
  91.2 3.7 %subtract_convert_fusion.1 = (bf16[1,1,512,512]{2,3,0,1:T(8,128)(2,1)S(1)}, bf16[1,1,512,512]{2,3,0,1:T(8,128)(2,1)S(1)}) fusion(f32[2,1,512,512]{2,3,0,1:T(8,128)} %convolution_bitcast_fusion, f32[]{:T(128)} %bitcast.27, f32[]{:T(128)} %bitcast.26, f32[]{:T(128)} %bitcast.30), kind=kLoop, calls=%fused_computation.16 | loop fusion | flops 2621440 | bytes 3145740 | tf_op jit(solution)/shard_map/convert.6
  95.1 1.0 copy.60
  96.1 22.5 %all_to_all.32 = bf16[2,1,512,512]{3,0,1,2:T(2,128)(2,1)S(1)} all-to-all(bf16[2,1,512,512]{3,0,1,2:T(2,128)(2,1)S(1)} %copy.60), channel_id=1, replica_groups=mesh['blk'=16,'pen'=32] {'pen'}, dimensions={2} | all-to-all | bytes 2097152 | tf_op jit(solution)/shard_map/all_to_all | solution.py:47
  118.5 1.1 copy.61
  (40 shorter events, 1.0 us)
Async XLA Ops:
  0.0 59.2 %copy-start = (bf16[1,2,512,512]{3,2,1,0:T(8,128)(2,1)S(1)}, bf16[1,2,512,512]{3,2,1,0:T(8,128)(2,1)}, u32[]{:S(2)}) copy-start(bf16[1,2,512,512]{3,2,1,0:T(8,128)(2,1)} %param.12) | copy-start | bytes 3145732
  0.0 12.9 %copy-start.6 = (s32[1,2]{1,0:T(1,128)S(1)}, s32[1,2]{1,0:T(1,128)}, u32[]{:S(2)}) copy-start(s32[1,2]{1,0:T(1,128)} %param.14) | copy-start | bytes 28
  0.0 16.0 %copy-start.7 = (s32[1,2]{1,0:T(1,128)S(1)}, s32[1,2]{1,0:T(1,128)}, u32[]{:S(2)}) copy-start(s32[1,2]{1,0:T(1,128)} %param.15) | copy-start | bytes 28
  0.0 21.6 %copy-start.8 = (s32[1,2]{1,0:T(1,128)S(1)}, s32[1,2]{1,0:T(1,128)}, u32[]{:S(2)}) copy-start(s32[1,2]{1,0:T(1,128)} %param.16) | copy-start | bytes 28
  0.0 23.4 %copy-start.9 = (s32[1,2]{1,0:T(1,128)S(1)}, s32[1,2]{1,0:T(1,128)}, u32[]{:S(2)}) copy-start(s32[1,2]{1,0:T(1,128)} %param.17) | copy-start | bytes 28
  0.0 25.4 %copy-start.2 = (f32[1,3]{1,0:T(1,128)S(1)}, f32[1,3]{1,0:T(1,128)}, u32[]{:S(2)}) copy-start(f32[1,3]{1,0:T(1,128)} %param.13) | copy-start | bytes 40
  2.4 27.5 %all-to-all-start = ((bf16[2,32,16,512]{3,2,0,1:T(8,128)(2,1)}), bf16[2,32,16,512]{3,2,0,1:T(8,128)(2,1)S(1)}, u32[]{:S(2)}, u32[]{:S(2)}) async-start(bf16[2,32,16,512]{3,2,0,1:T(8,128)(2,1)} %bitcast.97), calls=%async_computation | async-start | bytes 2097152 | tf_op jit(solution)/shard_map/all_to_all | solution.py:33
  25.3 32.0 %copy-start.4 = (pred[512]{0:T(512)(128)(4,1)}, pred[512]{0:T(512)(128)(4,1)S(1)}, u32[]{:S(2)}) copy-start(pred[512]{0:T(512)(128)(4,1)S(1)} %compare_and_fusion.1) | copy-start | bytes 1540
  31.0 24.6 %all-to-all-start.1 = ((bf16[16,1,2,2,1,512]{5,3,4,2,1,0:T(2,128)(2,1)}), bf16[16,1,2,2,1,512]{5,3,4,2,1,0:T(2,128)(2,1)S(1)}, u32[]{:S(2)}, u32[]{:S(2)}) async-start(bf16[16,1,2,2,1,512]{5,3,4,2,1,0:T(2,128)(2,1)} %stack.34), calls=%async_computation.1 | async-start | bytes 131072 | tf_op jit(solution)/shard_map/all_to_all | solution.py:11
  44.0 19.2 %copy-start.5 = (pred[512]{0:T(512)(128)(4,1)}, pred[512]{0:T(512)(128)(4,1)S(1)}, u32[]{:S(2)}) copy-start(pred[512]{0:T(512)(128)(4,1)S(1)} %compare_and_fusion) | copy-start | bytes 1540
  45.3 17.8 %copy-start.3 = (f32[2,512]{1,0:T(2,128)}, f32[2,512]{1,0:T(2,128)S(1)}, u32[]{:S(2)}) copy-start(f32[2,512]{1,0:T(2,128)S(1)} %get-tuple-element.7) | copy-start | bytes 12292
  66.9 20.4 %copy-start.1 = (bf16[1,2,512,512]{3,2,1,0:T(8,128)(2,1)S(1)}, bf16[1,2,512,512]{3,2,1,0:T(8,128)(2,1)}, u32[]{:S(2)}) copy-start(bf16[1,2,512,512]{3,2,1,0:T(8,128)(2,1)} %param.11) | copy-start | bytes 3145732
